TPU v7x, 512 devices: a whole 4x4x16 slice. The times are simulated.
512 devices in a mesh: ctx: 64 (over y, z), tp: 8 (over x, core).
Axes of the slice: x: 4, y: 4, z: 16, core: 2. Of those that a mesh axis runs over, the one named last changes fastest.
Arguments:
- query_rows: bfloat16 [32768, 4096], P('ctx', 'tp'), may hold values from -6 to 6
- key_rows: bfloat16 [32768, 4096], P('ctx', 'tp'), may hold values from -0.52734375 to 0.52734375
- value_rows: bfloat16 [32768, 4096], P('ctx', 'tp'), may hold values from -6 to 6
- log_decay: float32 [32, 32768], P('tp', 'ctx'), may hold values from -1 to 0
- norm_gain: float32 [4096], P('tp'), may hold values from 0.25 to 1.75
- out_weight: bfloat16 [4096, 3072], P(None, 'tp'), may hold values from -0.09375 to 0.09375
Outputs:
- projected: bfloat16 [32768, 3072], P('ctx', 'tp')
All inputs are finite; a program needn't handle non-finite values.
Results may differ from a plain program's by a relative error of at most 0.015.
Values may be sent and summed in bfloat16 or wider, within the bound.
A program may use at most 64 MiB of HBM per device.

v0:
```python
import jax
import jax.numpy as jnp
from jax import lax
from jax.sharding import PartitionSpec as P

HEADS = 32
HEAD_DIM = 128
BLOCK = 128


def entering_2(part, axis, combine, identity):
    place = lax.axis_index(axis)
    gathered = jax.tree.map(lambda a: lax.all_gather(a, axis), part)
    state = jax.tree.map(lambda a, e: jnp.zeros_like(a) + jnp.asarray(e, a.dtype), part, identity)

    def one(lap, state):
        return combine(
            state, jax.tree.map(lambda a: lax.dynamic_index_in_dim(a, lap, 0, False), gathered)
        )

    return lax.fori_loop(0, place, one, state)


def chain_combine(earlier, later):
    return (earlier[0] * later[0], later[0][:, None, None] * earlier[1] + later[1])


def incoming_from(shard_decay, shard_state):
    identity = (jnp.ones_like(shard_decay), jnp.zeros_like(shard_state))
    result = entering_2((shard_decay, shard_state), "ctx", chain_combine, identity)
    return result[1]


def split_parts(values):
    high = values.astype(jnp.bfloat16)
    low = (values - high.astype(jnp.float32)).astype(jnp.bfloat16)
    return (high, low)


def split_einsum(form, narrow, wide_first, wide_second):
    if narrow == 0:
        first = jnp.einsum(form, wide_first[0], wide_second, preferred_element_type=jnp.float32)
        second = jnp.einsum(form, wide_first[1], wide_second, preferred_element_type=jnp.float32)
    else:
        first = jnp.einsum(form, wide_first, wide_second[0], preferred_element_type=jnp.float32)
        second = jnp.einsum(form, wide_first, wide_second[1], preferred_element_type=jnp.float32)
    return first + second


def per_device(query_rows, key_rows, value_rows, log_decay, norm_gain, out_weight):
    length = query_rows.shape[0]
    feature_count = query_rows.shape[1]
    head_count = log_decay.shape[0]
    head_width = feature_count // head_count
    blocks = length // BLOCK
    q_block = query_rows.reshape(blocks, BLOCK, head_count, head_width)
    k_block = key_rows.reshape(blocks, BLOCK, head_count, head_width)
    v_block = value_rows.reshape(blocks, BLOCK, head_count, head_width)
    cum = jnp.cumsum(log_decay.reshape(head_count, blocks, BLOCK), axis=-1)
    causal = jnp.arange(BLOCK)[:, None] >= jnp.arange(BLOCK)[None, :]
    spread_log = cum[..., :, None] - cum[..., None, :]
    factor = jnp.where(causal, jnp.exp(jnp.where(causal, spread_log, 0.0)), 0.0)
    scores = jnp.einsum("bthe,bshe->hbts", q_block, k_block, preferred_element_type=jnp.float32)
    weights = (scores * factor).astype(jnp.bfloat16)
    inside_part = jnp.einsum(
        "hbts,bshe->bthe", weights, v_block, preferred_element_type=jnp.float32
    )
    to_end = jnp.transpose(jnp.exp(cum[..., -1:] - cum), (1, 2, 0))
    k_scaled = k_block.astype(jnp.float32) * to_end[..., None]
    block_states = split_einsum("bshe,bshf->bhef", 0, split_parts(k_scaled), v_block)
    block_totals = cum[..., -1]
    block_decay = jnp.exp(block_totals)
    offsets = jnp.cumsum(block_totals, axis=1) - block_totals
    running = jnp.zeros((head_count, head_width, head_width), jnp.float32)
    entering_list = []
    for index_block in range(blocks):
        entering_list.append(running)
        running = block_decay[:, index_block][:, None, None] * running + block_states[index_block]
    entering = jnp.stack(entering_list, axis=0)
    shard_decay = jnp.exp(jnp.sum(block_totals, axis=1))
    growth = jnp.transpose(jnp.exp(cum), (1, 2, 0))[..., None]
    incoming = incoming_from(shard_decay, running)
    entering_all = entering + jnp.transpose(jnp.exp(offsets))[:, :, None, None] * incoming[None]
    carried_part = split_einsum("bthe,bhef->bthf", 1, q_block, split_parts(entering_all)) * growth
    attention = inside_part + carried_part
    attention = attention.reshape(length, feature_count)
    squares = jnp.sum(attention * attention, axis=-1)
    summed = lax.psum(squares, "tp")
    scale = lax.rsqrt(summed / (HEADS * HEAD_DIM) + 1e-06)
    normed = (attention * scale[:, None] * norm_gain).astype(jnp.bfloat16)
    projected = jnp.dot(
        lax.all_gather(normed, "tp", axis=1, tiled=True),
        out_weight,
        preferred_element_type=jnp.float32,
    )
    return projected.astype(jnp.bfloat16)


def solution(mesh):
    in_specs = (
        P("ctx", "tp"),
        P("ctx", "tp"),
        P("ctx", "tp"),
        P("tp", "ctx"),
        P("tp"),
        P(None, "tp"),
    )
    out_specs = P("ctx", "tp")
    return jax.shard_map(
        per_device, mesh=mesh, in_specs=in_specs, out_specs=out_specs, check_vma=False
    )
```

profile of v0, /device:TPU:1, one launch (start us, length us, event | category | flops | bytes accessed | tf_op | source)
XLA Modules:
  0.0 353.3 jit_solution(14344379508308429635)
XLA Ops:
  6.5 0.0 copy-start
  6.5 0.0 all-gather.4.cloned.1.call-start
  6.5 0.9 reshape.42
  7.4 1.2 reduce_window_sum.24
  8.6 0.2 slice_reduce_fusion
  8.8 0.2 reduce_window_sum.26
  9.0 0.1 bitcast_exponential_fusion
  9.1 2.0 reshape.41
  11.0 2.1 copy.39
  13.1 2.0 reshape.43
  15.0 1.5 fusion.11
  16.5 1.5 convolution_add_fusion.1
  18.1 0.2 slice_reduce_fusion.2
  18.3 1.1 slice_add_fusion
  19.4 0.0 all-gather.4.cloned.1.call-update
  19.4 0.0 all-gather.6.cloned.1.call-start
  19.5 1.3 dynamic-slice
  21.3 0.1 exponential_dynamic-update-slice_fusion
  21.4 123.6 %all-reduce = f32[256]{0:T(256)S(1)} all-reduce(f32[256]{0:T(256)S(1)} %exponential_dynamic-update-slice_fusion), channel_id=2, replica_groups=mesh['ctx'=64,'tp'=8] {'ctx'}, use_global_device_ids=true, to_apply=%add | all-reduce | flops 256 | bytes 2048
  145.0 0.1 reshape.45
  145.1 0.1 copy.43
  145.2 2.0 reshape.40
  147.2 3.1 convolution_bitcast_fusion
  150.3 68.3 %all-gather.4.cloned.1.call-done = f32[64,4,128,128]{3,2,1,0:T(8,128)} async-done(((f32[1,4,128,128]{3,2,1,0:T(8,128)}), f32[64,4,128,128]{3,2,1,0:T(8,128)}) %all-gather.4.cloned.1.call-update) | async-done | bytes 16777232 | tf_op jit(solution)/shard_map/all_gather | solution.py:13
  218.7 0.0 copy-start.1
  218.7 1.9 fusion.27
  220.6 3.3 multiply_reduce_fusion
  223.9 2.5 copy.49
  226.5 12.7 %psum.7 = f32[512]{0:T(512)S(1)} all-reduce(f32[512]{0:T(512)S(1)} %bitcast.40), channel_id=1, replica_groups=mesh['ctx'=64,'tp'=8] {'tp'}, use_global_device_ids=true, to_apply=%region_6.7 | all-reduce | flops 512 | bytes 4096 | tf_op jit(solution)/shard_map/psum | solution.py:88
  239.2 0.0 copy-done.1
  239.2 2.2 fusion.5
  241.4 0.0 all-gather.6.cloned.1.call-update
  241.4 99.7 %all-gather.6.cloned.1.call-done = bf16[512,4096]{1,0:T(8,128)(2,1)} async-done(((bf16[512,512]{1,0:T(8,128)(2,1)}), bf16[512,4096]{1,0:T(8,128)(2,1)}) %all-gather.6.cloned.1.call-update) | async-done | bytes 4194320 | tf_op jit(solution)/shard_map/all_gather | solution.py:92
  341.2 0.0 copy-done
  341.2 5.3 %convolution_convert_fusion = bf16[512,384]{1,0:T(8,128)(2,1)} fusion(bf16[512,4096]{1,0:T(8,128)(2,1)} %all-gather.6.cloned.1.call-done, bf16[4096,384]{1,0:T(8,128)(2,1)S(1)} %copy-done), kind=kOutput, calls=%fused_computation.10 | convolution fusion | flops 1610809344 | bytes 7733248 | tf_op jit(solution)/shard_map/dot_general | solution.py:91
  (10 shorter events, 0.1 us)
Async XLA Ops:
  6.5 334.6 %copy-start = (bf16[4096,384]{1,0:T(8,128)(2,1)S(1)}, bf16[4096,384]{1,0:T(8,128)(2,1)}, u32[]{:S(2)}) copy-start(bf16[4096,384]{1,0:T(8,128)(2,1)} %param.13) | copy-start | bytes 9437188
  6.5 212.1 %all-gather.4.cloned.1.call-start = ((), (), s32[]{:S(2)}) async-start(), calls=%async_computation | async-start | bytes 17039360 | tf_op jit(solution)/shard_map/all_gather | solution.py:13
  19.4 321.8 %all-gather.6.cloned.1.call-start = ((), (), s32[]{:S(2)}) async-start(), calls=%async_computation.1 | async-start | bytes 4718592 | tf_op jit(solution)/shard_map/all_gather | solution.py:92
  218.7 20.6 %copy-start.1 = (f32[512]{0:T(512)S(1)}, f32[512]{0:T(512)}, u32[]{:S(2)}) copy-start(f32[512]{0:T(512)} %param.12) | copy-start | bytes 6148
Sparse Core Ops, SparseCore 0:
  19.5 199.0 all-gather.3
  241.6 99.5 all-gather.5
where the time goes:
time: 356 us; the launch traced here: 353 us
  waiting for transfers between devices  168 us (47%)
  blocking collectives  136 us (38%)
  matrix products  16.6 us (5%)
  between operations  14.1 us (4%)
  local copies, waits for them, and re-layouts  13 us (4%)
  other arithmetic  5.13 us (1%)
    unnamed x1, blocking collectives  124 us
    all_gather x1, waiting for transfers between devices, per_device(): lax.all_gather(normed, 'tp', axis=1, tiled=True)  99.7 us
    all_gather x1, waiting for transfers between devices, entering_2(): gathered = jax.tree.map(lambda a: lax.all_gather(a, axis), part)  68.3 us
    psum x1, blocking collectives, per_device(): summed = lax.psum(squares, 'tp')  12.7 us
  transfers between devices with their start and end apart: 2, of which 2 were waited for; matrix products, arithmetic and copies ran while one was open for 2% of the time, Pallas kernels for 0%

commit v1 on v0

v1 whole, which is shorter than its diff:
```python
import functools

import jax
import jax.numpy as jnp
from jax import lax
from jax.experimental import pallas as pl
from jax.experimental.pallas import tpu as pltpu
from jax.sharding import PartitionSpec as P

HEADS = 32
HEAD_DIM = 128
MESH = pl.DeviceIdType.MESH
F32 = jnp.float32
BF16 = jnp.bfloat16
LANES = 128
NZ = 16
NY = 4
NX = 4
FAR_FIRST = (8, 7, 9, 6, 10, 5, 11, 4, 12, 3, 13, 2, 14, 1, 15)


def dot(a, b, contract):
    return lax.dot_general(a, b, (contract, ((), ())), preferred_element_type=F32)


def column(row):
    return jnp.transpose(jnp.broadcast_to(row, (LANES, LANES)))


def kernel(
    q_hbm, k_hbm, v_hbm, ld_ref, gain_ref, w_hbm, out_ref,
    q_ref, k_ref, v_ref, w_ref, cum_ref, col_ref, att_ref, acc_ref,
    s_send, s_recv, d_send, d_recv, p_ref, p_log, t_send, t_recv, e_send, e_recv,
    p_send, i_ref, a_ref, ssq_ref,
    load_sem, s_ssem, s_rsem, d_ssem, d_rsem, t_ssem, t_rsem, e_ssem, e_rsem,
    p_ssem, p_rsem, q_ssem, q_rsem, r_ssem, l_ssem, c_ssem, a_rsem,
):
    heads, length = ld_ref.shape
    tiles = length // LANES
    ctx = lax.axis_index("ctx")
    tp = lax.axis_index("tp")
    y, z = ctx // NZ, lax.rem(ctx, NZ)
    x, core = tp // 2, lax.rem(tp, 2)

    def tp_at(dx, other):
        cx = lax.rem(x + dx, NX)
        cc = 1 - core if other else core
        return cx * 2 + cc

    def z_peer(i):
        return y * NZ + lax.rem(z + i, NZ)

    def y_peer(i):
        return lax.rem(y + i, NY) * NZ + z

    loads = [
        pltpu.make_async_copy(src, dst, load_sem.at[n])
        for n, (src, dst) in enumerate(
            ((k_hbm, k_ref), (v_hbm, v_ref), (q_hbm, q_ref), (w_hbm, w_ref))
        )
    ]
    for copy in loads:
        copy.start()

    barrier = pltpu.get_barrier_semaphore()
    for i in FAR_FIRST:
        pl.semaphore_signal(barrier, inc=1, device_id={"ctx": z_peer(i)}, device_id_type=MESH)
    for i in (2, 1, 3):
        pl.semaphore_signal(barrier, inc=1, device_id={"ctx": y_peer(i)}, device_id_type=MESH)
    tp_peers = [tp_at(dx, other) for dx in range(NX) for other in (False, True)][1:]
    for peer in tp_peers:
        pl.semaphore_signal(barrier, inc=1, device_id={"tp": peer}, device_id_type=MESH)

    steps = jnp.concatenate(
        [ld_ref[:, b * LANES : (b + 1) * LANES] for b in range(tiles)]
        + ([] if heads * tiles % 8 == 0 else [jnp.zeros((8 - heads * tiles % 8, LANES), F32)]),
        axis=0,
    )
    lane = lax.broadcasted_iota(jnp.int32, steps.shape, 1)
    shift = 1
    while shift < LANES:
        steps = steps + jnp.where(lane >= shift, pltpu.roll(steps, shift, 1), 0.0)
        shift *= 2
    before = jnp.zeros((heads, LANES), F32)
    for b in range(tiles):
        part = steps[b * heads : (b + 1) * heads, :] + before
        cum_ref[b * heads : (b + 1) * heads, :] = part
        before = jnp.broadcast_to(part[:, LANES - 1 :], (heads, LANES))
    for h in range(heads):
        d_send[h] = before[h : h + 1, :]

    loads[0].wait()
    loads[1].wait()
    for h in range(heads):
        span = slice(h * LANES, (h + 1) * LANES)
        total = d_send[h]
        pieces = []
        for b in range(tiles):
            rows = slice(b * LANES, (b + 1) * LANES)
            col = column(cum_ref[b * heads + h : b * heads + h + 1, :])
            col_ref[h, rows, :] = col
            pieces.append((k_ref[rows, span].astype(F32) * jnp.exp(total - col)).astype(BF16))
        scaled = jnp.concatenate(pieces, axis=0)
        state = dot(scaled, v_ref[:, span], ((0,), (0,)))
        s_send[h * 4 : (h + 1) * 4] = state.astype(BF16).reshape(4, 32, LANES)

    pl.semaphore_wait(barrier, (NZ - 1) + (NY - 1) + len(tp_peers))

    def s_copy(i):
        owner = lax.rem(z + i, NZ)
        return pltpu.make_async_remote_copy(
            src_ref=s_send.at[owner], dst_ref=s_recv.at[z], send_sem=s_ssem.at[i],
            recv_sem=s_rsem.at[i], device_id={"ctx": z_peer(i)}, device_id_type=MESH,
        )

    def d_copy(i):
        owner = lax.rem(z + i, NZ)
        return pltpu.make_async_remote_copy(
            src_ref=d_send.at[owner // 4], dst_ref=d_recv.at[z], send_sem=d_ssem.at[i],
            recv_sem=d_rsem.at[i], device_id={"ctx": z_peer(i)}, device_id_type=MESH,
        )

    for i in FAR_FIRST:
        d_copy(i).start()
        s_copy(i).start()
    s_recv[z] = s_send[z]
    d_recv[z] = d_send[z // 4]

    loads[2].wait()
    below = lax.broadcasted_iota(jnp.int32, (LANES, LANES), 0) >= lax.broadcasted_iota(
        jnp.int32, (LANES, LANES), 1
    )

    def inner_tile(h, b):
        span = slice(h * LANES, (h + 1) * LANES)
        rows = slice(b * LANES, (b + 1) * LANES)
        width = (b + 1) * LANES
        scores = dot(q_ref[rows, span], k_ref[:width, span], ((1,), (1,)))
        col = col_ref[h, rows, :]
        weights = []
        for s in range(b + 1):
            gap = col - cum_ref[s * heads + h : s * heads + h + 1, :]
            if s == b:
                factor = jnp.where(below, jnp.exp(jnp.where(below, gap, 0.0)), 0.0)
            else:
                factor = jnp.exp(gap)
            weights.append((scores[:, s * LANES : (s + 1) * LANES] * factor).astype(BF16))
        weight = weights[0] if b == 0 else jnp.concatenate(weights, axis=1)
        att_ref[rows, span] = dot(weight, v_ref[:width, span], ((1,), (0,)))

    for b in range(tiles):
        for h in range(heads):
            inner_tile(h, b)

    for i in FAR_FIRST:
        d_copy(i).wait_recv()
        s_copy(i).wait_recv()

    def scan_step(n, carry):
        state, log = carry
        p_ref[n] = state
        p_log[n] = log
        decay = d_recv[n]
        return jnp.exp(decay) * state + s_recv[n].astype(F32), log + decay

    state, log = lax.fori_loop(
        0, NZ, scan_step, (jnp.zeros((32, LANES), F32), jnp.zeros((1, LANES), F32)), unroll=True
    )
    t_send[...] = state
    e_send[...] = log

    def t_copy(i):
        return pltpu.make_async_remote_copy(
            src_ref=t_send, dst_ref=t_recv.at[y], send_sem=t_ssem.at[i],
            recv_sem=t_rsem.at[i], device_id={"ctx": y_peer(i)}, device_id_type=MESH,
        )

    def e_copy(i):
        return pltpu.make_async_remote_copy(
            src_ref=e_send, dst_ref=e_recv.at[y], send_sem=e_ssem.at[i],
            recv_sem=e_rsem.at[i], device_id={"ctx": y_peer(i)}, device_id_type=MESH,
        )

    for i in (2, 1, 3):
        e_copy(i).start()
        t_copy(i).start()
    t_recv[y] = state
    e_recv[y] = log
    for i in (1, 3, 2):
        e_copy(i).wait_recv()
        t_copy(i).wait_recv()
    entering = jnp.zeros((32, LANES), F32)
    for n in range(NY - 1):
        entering = jnp.where(n < y, jnp.exp(e_recv[n]) * entering + t_recv[n], entering)

    def p_copy(i):
        return pltpu.make_async_remote_copy(
            src_ref=p_send.at[lax.rem(z + i, NZ)], dst_ref=i_ref.at[z], send_sem=p_ssem.at[i],
            recv_sem=p_rsem.at[i], device_id={"ctx": z_peer(i)}, device_id_type=MESH,
        )

    for n in range(NZ):
        p_send[n] = (p_ref[n] + jnp.exp(p_log[n]) * entering).astype(BF16)
    for i in FAR_FIRST:
        p_copy(i).start()
    i_ref[z] = p_send[z]
    for i in FAR_FIRST:
        p_copy(i).wait_recv()

    for b in range(tiles):
        rows = slice(b * LANES, (b + 1) * LANES)
        squares = jnp.zeros((LANES, LANES), F32)
        for h in range(heads):
            span = slice(h * LANES, (h + 1) * LANES)
            state = i_ref[h * 4 : (h + 1) * 4].reshape(LANES, LANES)
            carried = dot(q_ref[rows, span], state, ((1,), (0,))) * jnp.exp(col_ref[h, rows, :])
            value = att_ref[rows, span] + carried
            squares = squares + value * value
            a_ref[tp, rows, span] = (value * gain_ref[:, span]).astype(BF16)
        ssq_ref[tp, :, rows] = jnp.sum(jnp.transpose(squares), axis=0, keepdims=True)

    def a_copy(slot, part, peer, ssem):
        rows = pl.ds(part * LANES, LANES)
        return pltpu.make_async_remote_copy(
            src_ref=a_ref.at[slot, rows], dst_ref=a_ref.at[slot, rows], send_sem=ssem,
            recv_sem=a_rsem.at[slot, part], device_id={"tp": peer}, device_id_type=MESH,
        )

    right, left, partner = tp_at(1, False), tp_at(NX - 1, False), tp_at(0, True)
    opposite = tp_at(2, False)
    right2, left2, opposite2 = tp_at(1, True), tp_at(NX - 1, True), tp_at(2, True)

    def ssq_copy(n):
        return pltpu.make_async_remote_copy(
            src_ref=ssq_ref.at[tp], dst_ref=ssq_ref.at[tp], send_sem=q_ssem.at[n],
            recv_sem=q_rsem.at[n], device_id={"tp": tp ^ (n + 1)}, device_id_type=MESH,
        )

    def ssq_from(n):
        slot = tp ^ (n + 1)
        return pltpu.make_async_remote_copy(
            src_ref=ssq_ref.at[slot], dst_ref=ssq_ref.at[slot], send_sem=q_ssem.at[n],
            recv_sem=q_rsem.at[n], device_id={"tp": slot}, device_id_type=MESH,
        )

    sent = []

    def start(slot, part, peer, ssem):
        copy = a_copy(slot, part, peer, ssem)
        copy.start()
        sent.append(copy)

    for n in range(7):
        ssq_copy(n).start()
    for r, l in zip((0, 1, 2, 3), (2, 3, 0, 1)):
        start(tp, r, right, r_ssem.at[r])
        start(tp, l, left, l_ssem.at[l])
        start(tp, r, partner, c_ssem.at[0, r])

    loads[3].wait()

    def project(slot, first=False):
        depth = a_ref.shape[2]
        product = dot(a_ref[slot], w_ref[pl.ds(pl.multiple_of(slot * depth, depth), depth), :], ((1,), (0,)))
        if first:
            acc_ref[...] = product
        else:
            acc_ref[...] += product

    def arrive(slot, part):
        a_copy(slot, part, partner, c_ssem.at[0, part]).wait_recv()

    project(tp, first=True)
    for r in range(tiles):
        arrive(partner, r)
    project(partner)
    for r, l in zip((0, 1, 2, 3), (2, 3, 0, 1)):
        arrive(left, r)
        if r < 2:
            start(left, r, right, r_ssem.at[4 + r])
        start(left, r, partner, c_ssem.at[1, r])
        arrive(right, l)
        if l >= 2:
            start(right, l, left, l_ssem.at[4 + l - 2])
        start(right, l, partner, c_ssem.at[2, l])
    project(left)
    project(right)
    for slot in (left2, right2):
        for r in range(tiles):
            arrive(slot, r)
        project(slot)
    for n in range(7):
        ssq_from(n).wait_recv()
    squares = ssq_ref[0]
    for n in range(1, 8):
        squares = squares + ssq_ref[n]
    scale = lax.rsqrt(squares / (HEADS * HEAD_DIM) + 1e-06)
    for r in (0, 2, 1, 3):
        arrive(opposite, r)
        start(opposite, r, partner, c_ssem.at[3, r])
    project(opposite)
    for r in (0, 2, 1, 3):
        arrive(opposite2, r)
    project(opposite2)
    for b in range(tiles):
        rows = slice(b * LANES, (b + 1) * LANES)
        col = column(scale[:, rows])
        for c in range(out_ref.shape[1] // LANES):
            cols = slice(c * LANES, (c + 1) * LANES)
            out_ref[rows, cols] = (acc_ref[rows, cols] * col).astype(BF16)

    for i in FAR_FIRST:
        d_copy(i).wait_send()
        s_copy(i).wait_send()
        p_copy(i).wait_send()
    for i in (1, 2, 3):
        e_copy(i).wait_send()
        t_copy(i).wait_send()
    for n in range(7):
        ssq_copy(n).wait_send()
    for copy in sent:
        copy.wait_send()


def per_device(query_rows, key_rows, value_rows, log_decay, norm_gain, out_weight):
    length, features = query_rows.shape
    heads = log_decay.shape[0]
    depth, width = out_weight.shape
    hbm = pl.BlockSpec(memory_space=pl.ANY)
    vmem = pl.BlockSpec(memory_space=pltpu.VMEM)
    dma = pltpu.SemaphoreType.DMA
    return pl.pallas_call(
        kernel,
        out_shape=jax.ShapeDtypeStruct((length, width), BF16),
        in_specs=[hbm, hbm, hbm, vmem, vmem, hbm],
        out_specs=vmem,
        scratch_shapes=[
            pltpu.VMEM((length, features), BF16),
            pltpu.VMEM((length, features), BF16),
            pltpu.VMEM((length, features), BF16),
            pltpu.VMEM((depth, width), BF16),
            pltpu.VMEM((16, LANES), F32),
            pltpu.VMEM((heads, length, LANES), F32),
            pltpu.VMEM((length, features), F32),
            pltpu.VMEM((length, width), F32),
            pltpu.VMEM((NZ, 32, LANES), BF16),
            pltpu.VMEM((NZ, 32, LANES), BF16),
            pltpu.VMEM((heads, 1, LANES), F32),
            pltpu.VMEM((NZ, 1, LANES), F32),
            pltpu.VMEM((NZ, 32, LANES), F32),
            pltpu.VMEM((NZ, 1, LANES), F32),
            pltpu.VMEM((32, LANES), F32),
            pltpu.VMEM((NY, 32, LANES), F32),
            pltpu.VMEM((1, LANES), F32),
            pltpu.VMEM((NY, 1, LANES), F32),
            pltpu.VMEM((NZ, 32, LANES), BF16),
            pltpu.VMEM((NZ, 32, LANES), BF16),
            pltpu.VMEM((8, length, features), BF16),
            pltpu.VMEM((8, 1, length), F32),
            dma((4,)),
            dma((NZ,)), dma((NZ,)), dma((NZ,)), dma((NZ,)),
            dma((NY,)), dma((NY,)), dma((NY,)), dma((NY,)),
            dma((NZ,)), dma((NZ,)),
            dma((7,)), dma((7,)),
            dma((6,)), dma((6,)), dma((4, 4)), dma((8, 4)),
        ],
        compiler_params=pltpu.CompilerParams(
            collective_id=0, has_side_effects=True, vmem_limit_bytes=48 * 1024 * 1024
        ),
        name="attention_layer",
    )(query_rows, key_rows, value_rows, log_decay, norm_gain.reshape(1, features), out_weight)


def solution(mesh):
    in_specs = (
        P("ctx", "tp"),
        P("ctx", "tp"),
        P("ctx", "tp"),
        P("tp", "ctx"),
        P("tp"),
        P(None, "tp"),
    )
    return jax.shard_map(
        per_device, mesh=mesh, in_specs=in_specs, out_specs=P("ctx", "tp"), check_vma=False
    )
```

time: 356 us -> 65.8 us (0.18)
  waiting for transfers between devices: 168 us -> 0 us
  blocking collectives: 136 us -> 0 us
  Pallas kernels: 0 us -> 58.3 us
  matrix products: 16.6 us -> 0 us
  between operations: 14.1 us -> 0.02 us
  local copies, waits for them, and re-layouts: 13 us -> 7.14 us
  other arithmetic: 5.13 us -> 0 us
    all_gather x2 -> x0, waiting for transfers between devices: 168 us -> none  [the longest x1 99.7 us: per_device(): lax.all_gather(normed, 'tp', axis=1, tiled=True)]
    unnamed x1 -> x0, blocking collectives: 124 us -> none
    pallas_call x0 -> x1, Pallas kernels: none -> 58.3 us  [per_device(): pl.pallas_call(kernel, out_shape=jax.ShapeDtypeStruct((length, width), BF...]
    dot_general x6 -> x0, matrix products: 16.6 us -> none  [the longest x1 5.26 us: per_device(): jnp.dot(lax.all_gather(normed, 'tp', axis=1, tiled=True), out_weight, pre...]
    psum x1 -> x0, blocking collectives: 12.7 us -> none  [per_device(): summed = lax.psum(squares, 'tp')]
    reshape x5 -> x0, local copies, waits for them, and re-layouts: 8.83 us -> none  [the longest x2 4.03 us: per_device(): k_block = key_rows.reshape(blocks, BLOCK, head_count, head_width)]
    unnamed x7 -> x13, local copies, waits for them, and re-layouts: 1.38 us -> 7.14 us
  transfers between devices with their start and end apart: 2 -> 0, of which waited for: 2 -> 0; matrix products, arithmetic and copies ran while one was open for 2% -> 0% of each run, Pallas kernels for 0% -> 0%
where the time goes in v1:
time: 65.8 us; the launch traced here: 65.4 us
  Pallas kernels  58.3 us (89%)
  local copies, waits for them, and re-layouts  7.14 us (11%)
    pallas_call x1, Pallas kernels, per_device(): pl.pallas_call(kernel, out_shape=jax.ShapeDtypeStruct((length, width), BF...  58.3 us
    unnamed x13, local copies, waits for them, and re-layouts  7.14 us

profile of v1, /device:TPU:1, one launch (start us, length us, event | category | flops | bytes accessed | tf_op | source)
XLA Modules:
  0.0 65.4 jit_solution(15604314239605737318)
XLA Ops:
  0.0 0.0 copy-start
  0.0 1.9 %copy-done = bf16[4096,384]{1,0:T(8,128)(2,1)S(1)} copy-done((bf16[4096,384]{1,0:T(8,128)(2,1)S(1)}, bf16[4096,384]{1,0:T(8,128)(2,1)}, u32[]{:S(2)}) %copy-start) | copy-done | bytes 3145752
  1.9 0.0 copy-start.1
  1.9 1.0 %copy-done.1 = bf16[512,512]{1,0:T(8,128)(2,1)S(1)} copy-done((bf16[512,512]{1,0:T(8,128)(2,1)S(1)}, bf16[512,512]{1,0:T(8,128)(2,1)}, u32[]{:S(2)}) %copy-start.1) | copy-done | bytes 524312
  2.9 0.0 copy-start.2
  2.9 1.0 %copy-done.2 = bf16[512,512]{1,0:T(8,128)(2,1)S(1)} copy-done((bf16[512,512]{1,0:T(8,128)(2,1)S(1)}, bf16[512,512]{1,0:T(8,128)(2,1)}, u32[]{:S(2)}) %copy-start.2) | copy-done | bytes 524312
  4.0 0.0 copy-start.3
  4.0 1.0 %copy-done.3 = bf16[512,512]{1,0:T(8,128)(2,1)S(1)} copy-done((bf16[512,512]{1,0:T(8,128)(2,1)S(1)}, bf16[512,512]{1,0:T(8,128)(2,1)}, u32[]{:S(2)}) %copy-start.3) | copy-done | bytes 524312
  5.0 0.0 copy-start.4
  5.0 0.7 %copy-done.4 = f32[4,512]{1,0:T(4,128)S(1)} copy-done((f32[4,512]{1,0:T(4,128)S(1)}, f32[4,512]{1,0:T(4,128)}, u32[]{:S(2)}) %copy-start.4) | copy-done | bytes 8216
  5.7 0.0 copy-start.5
  5.7 0.7 %copy-done.5 = f32[512]{0:T(512)S(1)} copy-done((f32[512]{0:T(512)S(1)}, f32[512]{0:T(512)}, u32[]{:S(2)}) %copy-start.5) | copy-done | bytes 2072
  6.4 58.3 %attention_layer.1 = bf16[512,384]{1,0:T(8,128)(2,1)S(1)} custom-call(bf16[512,512]{1,0:T(8,128)(2,1)S(1)} %copy-done.1, bf16[512,512]{1,0:T(8,128)(2,1)S(1)} %copy-done.2, bf16[512,512]{1,0:T(8,128)(2,1)S(1)} %copy-done.3, f32[4,512]{1,0:T(4,128)S(1)} %copy-done.4, f32[1,512]{1,0:T(1,128)S(1)} %bitcast.1, bf16[4096,384]{1,0:T(8,128)(2,1)S(1)} %copy-done), custom_call_target="tpu_custom_call" | custom-call | tf_op jit(solution)/shard_map/attention_layer/pallas_call | solution.py:332
  64.7 0.7 %copy.8 = bf16[512,384]{1,0:T(8,128)(2,1)} copy(bf16[512,384]{1,0:T(8,128)(2,1)S(1)} %attention_layer.1) | data formatting | bytes 786432
Async XLA Ops:
  0.0 1.9 %copy-start = (bf16[4096,384]{1,0:T(8,128)(2,1)S(1)}, bf16[4096,384]{1,0:T(8,128)(2,1)}, u32[]{:S(2)}) copy-start(bf16[4096,384]{1,0:T(8,128)(2,1)} %w_hbm.1) | copy-start | bytes 9437188
  1.9 1.0 %copy-start.1 = (bf16[512,512]{1,0:T(8,128)(2,1)S(1)}, bf16[512,512]{1,0:T(8,128)(2,1)}, u32[]{:S(2)}) copy-start(bf16[512,512]{1,0:T(8,128)(2,1)} %q_hbm.1) | copy-start | bytes 1572868
  2.9 1.0 %copy-start.2 = (bf16[512,512]{1,0:T(8,128)(2,1)S(1)}, bf16[512,512]{1,0:T(8,128)(2,1)}, u32[]{:S(2)}) copy-start(bf16[512,512]{1,0:T(8,128)(2,1)} %k_hbm.1) | copy-start | bytes 1572868
  4.0 1.0 %copy-start.3 = (bf16[512,512]{1,0:T(8,128)(2,1)S(1)}, bf16[512,512]{1,0:T(8,128)(2,1)}, u32[]{:S(2)}) copy-start(bf16[512,512]{1,0:T(8,128)(2,1)} %v_hbm.1) | copy-start | bytes 1572868
  5.0 0.7 %copy-start.4 = (f32[4,512]{1,0:T(4,128)S(1)}, f32[4,512]{1,0:T(4,128)}, u32[]{:S(2)}) copy-start(f32[4,512]{1,0:T(4,128)} %ld_ref.1) | copy-start | bytes 24580
  5.7 0.7 %copy-start.5 = (f32[512]{0:T(512)S(1)}, f32[512]{0:T(512)}, u32[]{:S(2)}) copy-start(f32[512]{0:T(512)} %param.10) | copy-start | bytes 6148

commit v2 on v1

v2 whole, which is shorter than its diff:
```python
import functools

import jax
import jax.numpy as jnp
from jax import lax
from jax.experimental import pallas as pl
from jax.experimental.pallas import tpu as pltpu
from jax.sharding import PartitionSpec as P

HEADS = 32
HEAD_DIM = 128
MESH = pl.DeviceIdType.MESH
F32 = jnp.float32
BF16 = jnp.bfloat16
LANES = 128
NZ = 16
NY = 4
NX = 4
EARLY = 320
FAR = (8, 7, 9, 6, 10, 5, 11)
NEAR = (4, 12, 3, 13, 2, 14, 1, 15)
FAR_FIRST = FAR + NEAR


def dot(a, b, contract):
    return lax.dot_general(a, b, (contract, ((), ())), preferred_element_type=F32)


def column(row):
    return jnp.transpose(jnp.broadcast_to(row, (LANES, LANES)))


def kernel(
    q_hbm, k_hbm, v_hbm, ld_hbm, gain_hbm, w_hbm, out_ref,
    ld_ref, gain_ref, q_ref, k_ref, v_ref, w_ref, cum_ref, col_ref, att_ref, acc_ref,
    s_send, s_recv, d_send, d_recv, sf_ref, df_ref, p_ref, t_send, t_recv, e_send, e_recv,
    p_send, i_ref, qt_ref, al_ref, g_ref, a_ref, own_ref, sq_ref, ssq_ref,
    load_sem, s_ssem, s_rsem, d_ssem, d_rsem, sf_ssem, sf_rsem, df_ssem, df_rsem, t_ssem, t_rsem, e_ssem, e_rsem,
    p_ssem, p_rsem, q_ssem, q_rsem, x_ssem, x_rsem,
):
    heads, length = ld_ref.shape
    tiles = length // LANES
    ctx = lax.axis_index("ctx")
    tp = lax.axis_index("tp")
    y, z = ctx // NZ, lax.rem(ctx, NZ)
    x, core = tp // 2, lax.rem(tp, 2)

    def tp_at(dx, other):
        cx = lax.rem(x + dx, NX)
        cc = 1 - core if other else core
        return cx * 2 + cc

    def z_peer(i):
        return y * NZ + lax.rem(z + i, NZ)

    def y_peer(i):
        return lax.rem(y + i, NY) * NZ + z

    barrier = pltpu.get_barrier_semaphore()
    for i in NEAR:
        pl.semaphore_signal(barrier, inc=1, device_id={"ctx": z_peer(i)}, device_id_type=MESH)
    for i in (2, 1, 3):
        pl.semaphore_signal(barrier, inc=1, device_id={"ctx": y_peer(i)}, device_id_type=MESH)
    tp_peers = [tp_at(dx, other) for dx in range(NX) for other in (False, True)][1:]
    for peer in tp_peers:
        pl.semaphore_signal(barrier, inc=1, device_id={"tp": peer}, device_id_type=MESH)

    loads = [
        pltpu.make_async_copy(src, dst, load_sem.at[n])
        for n, (src, dst) in enumerate(
            (
                (k_hbm, k_ref), (v_hbm, v_ref), (q_hbm, q_ref), (w_hbm, w_ref),
                (ld_hbm, ld_ref), (gain_hbm, gain_ref),
            )
        )
    ]
    for n in (4, 0, 1, 2, 5):
        loads[n].start()
    waiting = [4, 0, 1, 2, 5]
    sent = []

    def need(n):
        loads[n].wait()
        waiting.remove(n)

    def go(copy):
        copy.start()
        sent.append(copy)

    need(4)
    steps = jnp.concatenate(
        [ld_ref[:, b * LANES : (b + 1) * LANES] for b in range(tiles)]
        + ([] if heads * tiles % 8 == 0 else [jnp.zeros((8 - heads * tiles % 8, LANES), F32)]),
        axis=0,
    )
    lane = lax.broadcasted_iota(jnp.int32, steps.shape, 1)
    shift = 1
    while shift < LANES:
        steps = steps + jnp.where(lane >= shift, pltpu.roll(steps, shift, 1), 0.0)
        shift *= 2
    before = jnp.zeros((heads, LANES), F32)
    for b in range(tiles):
        part = steps[b * heads : (b + 1) * heads, :] + before
        cum_ref[b * heads : (b + 1) * heads, :] = part
        before = jnp.broadcast_to(part[:, LANES - 1 :], (heads, LANES))
    for h in range(heads):
        d_send[h] = before[h : h + 1, :]

    need(0)
    need(1)
    for h in range(heads):
        span = slice(h * LANES, (h + 1) * LANES)
        total = d_send[h]
        pieces = []
        for b in range(tiles):
            rows = slice(b * LANES, (b + 1) * LANES)
            col = column(cum_ref[b * heads + h : b * heads + h + 1, :])
            col_ref[h, rows, :] = col
            pieces.append((k_ref[rows, span].astype(F32) * jnp.exp(total - col)).astype(BF16))
        scaled = jnp.concatenate(pieces, axis=0)
        state = dot(scaled, v_ref[:, span], ((0,), (0,)))
        s_send[h * 4 : (h + 1) * 4] = state.astype(BF16).reshape(4, 32, LANES)

    need(2)
    for h in range(heads):
        span = slice(h * LANES, (h + 1) * LANES)
        growth = jnp.exp(col_ref[h, :EARLY, :])
        qt_ref[tp, :, span] = (q_ref[:EARLY, span].astype(F32) * growth).astype(BF16)

    pl.semaphore_wait(barrier, len(NEAR) + (NY - 1) + len(tp_peers))

    def s_copy(i):
        owner = lax.rem(z + i, NZ)
        return pltpu.make_async_remote_copy(
            src_ref=s_send.at[owner], dst_ref=s_recv.at[z], send_sem=s_ssem.at[i],
            recv_sem=s_rsem.at[i], device_id={"ctx": z_peer(i)}, device_id_type=MESH,
        )

    def d_copy(i):
        owner = lax.rem(z + i, NZ)
        return pltpu.make_async_remote_copy(
            src_ref=d_send.at[owner // 4], dst_ref=d_recv.at[z], send_sem=d_ssem.at[i],
            recv_sem=d_rsem.at[i], device_id={"ctx": z_peer(i)}, device_id_type=MESH,
        )

    def via(i):
        return 4 if i <= 8 else NZ - 4

    def s_out(i):
        return pltpu.make_async_remote_copy(
            src_ref=s_send.at[lax.rem(z + i, NZ)], dst_ref=sf_ref.at[i - 5],
            send_sem=s_ssem.at[i], recv_sem=sf_rsem.at[i - 5],
            device_id={"ctx": z_peer(via(i))}, device_id_type=MESH,
        )

    def d_out(i):
        return pltpu.make_async_remote_copy(
            src_ref=d_send.at[lax.rem(z + i, NZ) // 4], dst_ref=df_ref.at[i - 5],
            send_sem=d_ssem.at[i], recv_sem=df_rsem.at[i - 5],
            device_id={"ctx": z_peer(via(i))}, device_id_type=MESH,
        )

    def s_on(i):
        return pltpu.make_async_remote_copy(
            src_ref=sf_ref.at[i - 5], dst_ref=s_recv.at[lax.rem(z + NZ - via(i), NZ)],
            send_sem=sf_ssem.at[i - 5], recv_sem=s_rsem.at[i],
            device_id={"ctx": z_peer(NZ - via(i) + i)}, device_id_type=MESH,
        )

    def d_on(i):
        return pltpu.make_async_remote_copy(
            src_ref=df_ref.at[i - 5], dst_ref=d_recv.at[lax.rem(z + NZ - via(i), NZ)],
            send_sem=df_ssem.at[i - 5], recv_sem=d_rsem.at[i],
            device_id={"ctx": z_peer(NZ - via(i) + i)}, device_id_type=MESH,
        )

    for i in FAR:
        go(d_out(i))
        go(s_out(i))
    for i in NEAR:
        go(d_copy(i))
        go(s_copy(i))
    loads[3].start()
    waiting.append(3)
    s_recv[z] = s_send[z]
    d_recv[z] = d_send[z // 4]

    right, left, partner = tp_at(1, False), tp_at(NX - 1, False), tp_at(0, True)
    opposite = tp_at(2, False)
    right2, left2, opposite2 = tp_at(1, True), tp_at(NX - 1, True), tp_at(2, True)

    class Flow:
        def __init__(self, kind, ref):
            self.kind, self.ref, self.half, self.count = kind, ref, ref.shape[1] // 2, 0

        def copy(self, slot, part, peer, number):
            view = self.ref.at[slot, pl.ds(part * self.half, self.half)]
            return pltpu.make_async_remote_copy(
                src_ref=view, dst_ref=view, send_sem=x_ssem.at[self.kind, number],
                recv_sem=x_rsem.at[self.kind, slot, part], device_id={"tp": peer},
                device_id_type=MESH,
            )

        def start(self, slot, part, peer):
            go(self.copy(slot, part, peer, self.count))
            self.count += 1

        def arrive(self, slot, part):
            self.copy(slot, part, partner, 0).wait_recv()

        def own(self):
            for r, l in ((0, 1), (1, 0)):
                self.start(tp, r, right)
                self.start(tp, l, left)
            for part in (0, 1):
                self.start(tp, part, partner)

        def first(self):
            self.arrive(left, 0)
            self.start(left, 0, right)
            self.start(left, 0, partner)
            self.arrive(right, 1)
            self.start(right, 1, left)
            self.start(right, 1, partner)

        def second(self):
            self.arrive(left, 1)
            self.start(left, 1, partner)
            self.arrive(right, 0)
            self.start(right, 0, partner)

        def last(self):
            for part in (0, 1):
                self.arrive(opposite, part)
                self.start(opposite, part, partner)

        def near(self, slot):
            for part in (0, 1):
                self.arrive(slot, part)

    q_flow, al_flow, g_flow, a_flow = (
        Flow(n, ref) for n, ref in enumerate((qt_ref, al_ref, g_ref, a_ref))
    )
    q_flow.own()

    below = lax.broadcasted_iota(jnp.int32, (LANES, LANES), 0) >= lax.broadcasted_iota(
        jnp.int32, (LANES, LANES), 1
    )

    def inner_tile(h, b):
        span = slice(h * LANES, (h + 1) * LANES)
        rows = slice(b * LANES, (b + 1) * LANES)
        width = (b + 1) * LANES
        scores = dot(q_ref[rows, span], k_ref[:width, span], ((1,), (1,)))
        col = col_ref[h, rows, :]
        weights = []
        for s in range(b + 1):
            gap = col - cum_ref[s * heads + h : s * heads + h + 1, :]
            if s == b:
                factor = jnp.where(below, jnp.exp(jnp.where(below, gap, 0.0)), 0.0)
            else:
                factor = jnp.exp(gap)
            weights.append((scores[:, s * LANES : (s + 1) * LANES] * factor).astype(BF16))
        weight = weights[0] if b == 0 else jnp.concatenate(weights, axis=1)
        att_ref[rows, span] = dot(weight, v_ref[:width, span], ((1,), (0,)))

    for b in range(tiles):
        for h in range(heads):
            inner_tile(h, b)
    need(5)
    al_ref[tp] = (att_ref[:EARLY, :] * gain_ref[...]).astype(BF16)
    al_flow.own()

    for i in FAR:
        d_out(i).wait_recv()
        go(d_on(i))
        s_out(i).wait_recv()
        go(s_on(i))

    for i in FAR_FIRST:
        d_copy(i).wait_recv()
    log = jnp.zeros((1, LANES), F32)
    reach, decays = [], []
    for n in range(NZ):
        reach.append(jnp.exp(log))
        decays.append(jnp.exp(d_recv[n]))
        log = log + d_recv[n]
    e_send[...] = log

    def t_copy(i):
        return pltpu.make_async_remote_copy(
            src_ref=t_send, dst_ref=t_recv.at[y], send_sem=t_ssem.at[i],
            recv_sem=t_rsem.at[i], device_id={"ctx": y_peer(i)}, device_id_type=MESH,
        )

    def e_copy(i):
        return pltpu.make_async_remote_copy(
            src_ref=e_send, dst_ref=e_recv.at[y], send_sem=e_ssem.at[i],
            recv_sem=e_rsem.at[i], device_id={"ctx": y_peer(i)}, device_id_type=MESH,
        )

    for i in (2, 1, 3):
        go(e_copy(i))
    e_recv[y] = log
    for i in FAR_FIRST:
        s_copy(i).wait_recv()
    state = jnp.zeros((32, LANES), F32)
    prefixes = []
    for n in range(NZ):
        prefixes.append(state)
        state = decays[n] * state + s_recv[n].astype(F32)
    t_send[...] = state
    for i in (2, 1, 3):
        go(t_copy(i))
    t_recv[y] = state
    for n in range(NZ):
        p_ref[n] = prefixes[n]
    q_flow.first()
    for i in (1, 3, 2):
        e_copy(i).wait_recv()
    row_decays = [jnp.exp(e_recv[n]) for n in range(NY - 1)]
    for i in (1, 3, 2):
        t_copy(i).wait_recv()
    entering = jnp.zeros((32, LANES), F32)
    for n in range(NY - 1):
        entering = jnp.where(n < y, row_decays[n] * entering + t_recv[n], entering)

    def p_copy(i):
        return pltpu.make_async_remote_copy(
            src_ref=p_send.at[lax.rem(z + i, NZ)], dst_ref=i_ref.at[z], send_sem=p_ssem.at[i],
            recv_sem=p_rsem.at[i], device_id={"ctx": z_peer(i)}, device_id_type=MESH,
        )

    for n in range(NZ):
        p_send[n] = (p_ref[n] + reach[n] * entering).astype(BF16)
    for i in FAR_FIRST:
        go(p_copy(i))
    i_ref[z] = p_send[z]

    depth, width = a_ref.shape[2], out_ref.shape[1]
    early, late = slice(0, EARLY), slice(EARLY, length)

    def weight_of(slot):
        return w_ref[pl.ds(pl.multiple_of(slot * depth, depth), depth), :]

    def add(rows, block, slot):
        acc_ref[rows, :] += dot(block, weight_of(slot), ((1,), (0,)))

    def add_inner(slot):
        add(early, al_ref[slot], slot)

    def add_carried(slot):
        parts = []
        for h in range(heads):
            span = slice(h * LANES, (h + 1) * LANES)
            parts.append(
                dot(qt_ref[slot, :, span], g_ref[slot, span, :], ((1,), (0,))).astype(BF16)
            )
        add(early, jnp.concatenate(parts, axis=1), slot)

    def add_late(slot):
        add(late, a_ref[slot], slot)

    q_flow.second()
    acc_ref[...] = jnp.zeros_like(acc_ref)
    need(3)
    q_flow.near(partner)
    al_flow.near(partner)
    add_inner(partner)
    al_flow.first()
    al_flow.second()
    add_inner(left)
    add_inner(right)
    for slot in (left2, right2):
        q_flow.near(slot)
        al_flow.near(slot)
        add_inner(slot)
    q_flow.last()

    for i in FAR_FIRST:
        p_copy(i).wait_recv()
    for h in range(heads):
        span = slice(h * LANES, (h + 1) * LANES)
        state = i_ref[h * 4 : (h + 1) * 4].reshape(LANES, LANES).astype(F32)
        g_ref[tp, span, :] = (state * gain_ref[:, span]).astype(BF16)
    g_flow.own()

    def finish(rows, store):
        squares = None
        for h in range(heads):
            span = slice(h * LANES, (h + 1) * LANES)
            state = i_ref[h * 4 : (h + 1) * 4].reshape(LANES, LANES)
            carried = dot(q_ref[rows, span], state, ((1,), (0,))) * jnp.exp(col_ref[h, rows, :])
            value = att_ref[rows, span] + carried
            squares = value * value if squares is None else squares + value * value
            store(span, (value * gain_ref[:, span]).astype(BF16))
        sq_ref[rows, :] = squares

    def store_late(span, value):
        a_ref[tp, :, span] = value

    def store_own(span, value):
        own_ref[:, span] = value

    finish(late, store_late)
    a_flow.own()
    finish(early, store_own)
    for b in range(tiles):
        rows = slice(b * LANES, (b + 1) * LANES)
        ssq_ref[tp, :, rows] = jnp.sum(jnp.transpose(sq_ref[rows, :]), axis=0, keepdims=True)

    def ssq_copy(n):
        return pltpu.make_async_remote_copy(
            src_ref=ssq_ref.at[tp], dst_ref=ssq_ref.at[tp], send_sem=q_ssem.at[n],
            recv_sem=q_rsem.at[n], device_id={"tp": tp ^ (n + 1)}, device_id_type=MESH,
        )

    def ssq_from(n):
        slot = tp ^ (n + 1)
        return pltpu.make_async_remote_copy(
            src_ref=ssq_ref.at[slot], dst_ref=ssq_ref.at[slot], send_sem=q_ssem.at[n],
            recv_sem=q_rsem.at[n], device_id={"tp": slot}, device_id_type=MESH,
        )

    for n in range(7):
        go(ssq_copy(n))
    add(early, own_ref[...], tp)
    add_late(tp)
    g_flow.near(partner)
    add_carried(partner)
    al_flow.last()
    g_flow.first()
    g_flow.second()
    a_flow.near(partner)
    add_late(partner)
    add_carried(left)
    add_carried(right)
    a_flow.first()
    a_flow.second()
    add_late(left)
    add_late(right)
    g_flow.last()
    add_inner(opposite)
    add_carried(opposite)
    for slot in (left2, right2, opposite2):
        if slot is opposite2:
            q_flow.near(slot)
            al_flow.near(slot)
            add_inner(slot)
        g_flow.near(slot)
        add_carried(slot)
        if slot is not opposite2:
            a_flow.near(slot)
            add_late(slot)
    for n in range(7):
        ssq_from(n).wait_recv()
    squares = ssq_ref[0]
    for n in range(1, 8):
        squares = squares + ssq_ref[n]
    scale = lax.rsqrt(squares / (HEADS * HEAD_DIM) + 1e-06)
    a_flow.last()
    add_late(opposite)
    a_flow.near(opposite2)
    add_late(opposite2)
    for b in range(tiles):
        rows = slice(b * LANES, (b + 1) * LANES)
        out_ref[rows, :] = (acc_ref[rows, :] * jnp.tile(column(scale[:, rows]), (1, width // LANES))).astype(BF16)

    for n in waiting:
        loads[n].wait()
    for copy in sent:
        copy.wait_send()


def per_device(query_rows, key_rows, value_rows, log_decay, norm_gain, out_weight):
    length, features = query_rows.shape
    heads = log_decay.shape[0]
    depth, width = out_weight.shape
    hbm = pl.BlockSpec(memory_space=pltpu.HBM)
    vmem = pl.BlockSpec(memory_space=pltpu.VMEM)
    dma = pltpu.SemaphoreType.DMA
    return pl.pallas_call(
        kernel,
        out_shape=jax.ShapeDtypeStruct((length, width), BF16),
        in_specs=[hbm] * 6,
        out_specs=vmem,
        scratch_shapes=[
            pltpu.VMEM((heads, length), F32),
            pltpu.VMEM((1, features), F32),
            pltpu.VMEM((length, features), BF16),
            pltpu.VMEM((length, features), BF16),
            pltpu.VMEM((length, features), BF16),
            pltpu.VMEM((depth, width), BF16),
            pltpu.VMEM((16, LANES), F32),
            pltpu.VMEM((heads, length, LANES), F32),
            pltpu.VMEM((length, features), F32),
            pltpu.VMEM((length, width), F32),
            pltpu.VMEM((NZ, 32, LANES), BF16),
            pltpu.VMEM((NZ, 32, LANES), BF16),
            pltpu.VMEM((heads, 1, LANES), F32),
            pltpu.VMEM((NZ, 1, LANES), F32),
            pltpu.VMEM((7, 32, LANES), BF16),
            pltpu.VMEM((7, 1, LANES), F32),
            pltpu.VMEM((NZ, 32, LANES), F32),
            pltpu.VMEM((32, LANES), F32),
            pltpu.VMEM((NY, 32, LANES), F32),
            pltpu.VMEM((1, LANES), F32),
            pltpu.VMEM((NY, 1, LANES), F32),
            pltpu.VMEM((NZ, 32, LANES), BF16),
            pltpu.VMEM((NZ, 32, LANES), BF16),
            pltpu.VMEM((8, EARLY, features), BF16),
            pltpu.VMEM((8, EARLY, features), BF16),
            pltpu.VMEM((8, features, LANES), BF16),
            pltpu.VMEM((8, length - EARLY, features), BF16),
            pltpu.VMEM((EARLY, features), BF16),
            pltpu.VMEM((length, LANES), F32),
            pltpu.VMEM((8, 1, length), F32),
            dma((6,)),
            dma((NZ,)), dma((NZ,)), dma((NZ,)), dma((NZ,)),
            dma((7,)), dma((7,)), dma((7,)), dma((7,)),
            dma((NY,)), dma((NY,)), dma((NY,)), dma((NY,)),
            dma((NZ,)), dma((NZ,)),
            dma((7,)), dma((7,)),
            dma((4, 14)), dma((4, 8, 2)),
        ],
        compiler_params=pltpu.CompilerParams(
            collective_id=0, has_side_effects=True, vmem_limit_bytes=66650000
        ),
        name="attention_layer",
    )(query_rows, key_rows, value_rows, log_decay, norm_gain.reshape(1, features), out_weight)


def solution(mesh):
    in_specs = (
        P("ctx", "tp"),
        P("ctx", "tp"),
        P("ctx", "tp"),
        P("tp", "ctx"),
        P("tp"),
        P(None, "tp"),
    )
    return jax.shard_map(
        per_device, mesh=mesh, in_specs=in_specs, out_specs=P("ctx", "tp"), check_vma=False
    )
```

time: 65.8 us -> 56 us (0.85)
  local copies, waits for them, and re-layouts: 7.14 us -> 1.78 us
  Pallas kernels: 58.3 us -> 54 us
    unnamed x13 -> x1, local copies, waits for them, and re-layouts: 7.14 us -> 1.78 us
    pallas_call x1, Pallas kernels: 58.3 us -> 54 us  [per_device(): pl.pallas_call(kernel, out_shape=jax.ShapeDtypeStruct((length, width), BF...]
where the time goes in v2:
time: 56 us; the launch traced here: 55.8 us
  Pallas kernels  54 us (96%)
  local copies, waits for them, and re-layouts  1.78 us (3%)
    pallas_call x1, Pallas kernels, per_device(): pl.pallas_call(kernel, out_shape=jax.ShapeDtypeStruct((length, width), BF...  54 us
    unnamed x1, local copies, waits for them, and re-layouts  1.78 us

profile of v2, /device:TPU:1, one launch (start us, length us, event | category | flops | bytes accessed | tf_op | source)
XLA Modules:
  0.0 55.8 jit_solution(14813952828716927602)
XLA Ops:
  0.0 54.0 %attention_layer.1 = bf16[512,384]{1,0:T(8,128)(2,1)} custom-call(bf16[512,512]{1,0:T(8,128)(2,1)} %q_hbm.1, bf16[512,512]{1,0:T(8,128)(2,1)} %k_hbm.1, bf16[512,512]{1,0:T(8,128)(2,1)} %v_hbm.1, f32[4,512]{1,0:T(4,128)} %ld_hbm.1, f32[1,512]{1,0:T(1,128)} %bitcast.1, bf16[4096,384]{1,0:T(8,128)(2,1)} %w_hbm.1), custom_call_target="tpu_custom_call" | custom-call | tf_op jit(solution)/shard_map/attention_layer/pallas_call | solution.py:482
  54.0 1.8 %copy.8 = bf16[512,384]{1,0:T(8,128)(2,1)} copy(bf16[512,384]{1,0:T(8,128)(2,1)} %attention_layer.1) | data formatting | bytes 786432

commit v3 on v2

--- a/solution.py
+++ b/solution.py
@@ -16,7 +16,7 @@
 NZ = 16
 NY = 4
 NX = 4
-EARLY = 320
+EARLY = 288
 FAR = (8, 7, 9, 6, 10, 5, 11)
 NEAR = (4, 12, 3, 13, 2, 14, 1, 15)
 FAR_FIRST = FAR + NEAR
@@ -31,11 +31,11 @@
 
 
 def kernel(
-    q_hbm, k_hbm, v_hbm, ld_hbm, gain_hbm, w_hbm, out_ref,
-    ld_ref, gain_ref, q_ref, k_ref, v_ref, w_ref, cum_ref, col_ref, att_ref, acc_ref,
+    q_hbm, k_hbm, v_hbm, ld_hbm, gain_hbm, w_hbm, out_hbm,
+    out_ref, ld_ref, gain_ref, q_ref, k_ref, v_ref, w_ref, cum_ref, col_ref, att_ref, acc_ref,
     s_send, s_recv, d_send, d_recv, sf_ref, df_ref, p_ref, t_send, t_recv, e_send, e_recv,
     p_send, i_ref, qt_ref, al_ref, g_ref, a_ref, own_ref, sq_ref, ssq_ref,
-    load_sem, s_ssem, s_rsem, d_ssem, d_rsem, sf_ssem, sf_rsem, df_ssem, df_rsem, t_ssem, t_rsem, e_ssem, e_rsem,
+    out_sem, load_sem, s_ssem, s_rsem, d_ssem, d_rsem, sf_ssem, sf_rsem, df_ssem, df_rsem, t_ssem, t_rsem, e_ssem, e_rsem,
     p_ssem, p_rsem, q_ssem, q_rsem, x_ssem, x_rsem,
 ):
     heads, length = ld_ref.shape
@@ -56,6 +56,17 @@
     def y_peer(i):
         return lax.rem(y + i, NY) * NZ + z
 
+    loads = [
+        pltpu.make_async_copy(src, dst, load_sem.at[n])
+        for n, (src, dst) in enumerate(
+            (
+                (k_hbm, k_ref), (v_hbm, v_ref), (q_hbm, q_ref), (w_hbm, w_ref),
+                (ld_hbm, ld_ref), (gain_hbm, gain_ref),
+            )
+        )
+    ]
+    for n in (4, 0, 1):
+        loads[n].start()
     barrier = pltpu.get_barrier_semaphore()
     for i in NEAR:
         pl.semaphore_signal(barrier, inc=1, device_id={"ctx": z_peer(i)}, device_id_type=MESH)
@@ -65,16 +76,7 @@
     for peer in tp_peers:
         pl.semaphore_signal(barrier, inc=1, device_id={"tp": peer}, device_id_type=MESH)
 
-    loads = [
-        pltpu.make_async_copy(src, dst, load_sem.at[n])
-        for n, (src, dst) in enumerate(
-            (
-                (k_hbm, k_ref), (v_hbm, v_ref), (q_hbm, q_ref), (w_hbm, w_ref),
-                (ld_hbm, ld_ref), (gain_hbm, gain_ref),
-            )
-        )
-    ]
-    for n in (4, 0, 1, 2, 5):
+    for n in (2, 5):
         loads[n].start()
     waiting = [4, 0, 1, 2, 5]
     sent = []
@@ -121,12 +123,6 @@
         state = dot(scaled, v_ref[:, span], ((0,), (0,)))
         s_send[h * 4 : (h + 1) * 4] = state.astype(BF16).reshape(4, 32, LANES)
 
-    need(2)
-    for h in range(heads):
-        span = slice(h * LANES, (h + 1) * LANES)
-        growth = jnp.exp(col_ref[h, :EARLY, :])
-        qt_ref[tp, :, span] = (q_ref[:EARLY, span].astype(F32) * growth).astype(BF16)
-
     pl.semaphore_wait(barrier, len(NEAR) + (NY - 1) + len(tp_peers))
 
     def s_copy(i):
@@ -241,6 +237,12 @@
     q_flow, al_flow, g_flow, a_flow = (
         Flow(n, ref) for n, ref in enumerate((qt_ref, al_ref, g_ref, a_ref))
     )
+    need(2)
+    for h in range(heads):
+        span = slice(h * LANES, (h + 1) * LANES)
+        growth = jnp.exp(col_ref[h, :EARLY, :])
+        qt_ref[tp, :, span] = (q_ref[:EARLY, span].astype(F32) * growth).astype(BF16)
+
     q_flow.own()
 
     below = lax.broadcasted_iota(jnp.int32, (LANES, LANES), 0) >= lax.broadcasted_iota(
@@ -428,9 +430,9 @@
     add_late(tp)
     g_flow.near(partner)
     add_carried(partner)
-    al_flow.last()
     g_flow.first()
     g_flow.second()
+    al_flow.last()
     a_flow.near(partner)
     add_late(partner)
     add_carried(left)
@@ -442,6 +444,26 @@
     g_flow.last()
     add_inner(opposite)
     add_carried(opposite)
+    for n in range(7):
+        ssq_from(n).wait_recv()
+    squares = ssq_ref[0]
+    for n in range(1, 8):
+        squares = squares + ssq_ref[n]
+    scale = lax.rsqrt(squares / (HEADS * HEAD_DIM) + 1e-06)
+    for b in range(tiles):
+        rows = slice(b * LANES, (b + 1) * LANES)
+        sq_ref[rows, :] = column(scale[:, rows])
+
+    def out_copy(rows, n):
+        view = pl.ds(rows.start, rows.stop - rows.start)
+        return pltpu.make_async_copy(out_ref.at[view], out_hbm.at[view], out_sem.at[n])
+
+    def write(rows, n):
+        out_ref[rows, :] = (
+            acc_ref[rows, :] * jnp.tile(sq_ref[rows, :], (1, width // LANES))
+        ).astype(BF16)
+        out_copy(rows, n).start()
+
     for slot in (left2, right2, opposite2):
         if slot is opposite2:
             q_flow.near(slot)
@@ -452,24 +474,19 @@
         if slot is not opposite2:
             a_flow.near(slot)
             add_late(slot)
-    for n in range(7):
-        ssq_from(n).wait_recv()
-    squares = ssq_ref[0]
-    for n in range(1, 8):
-        squares = squares + ssq_ref[n]
-    scale = lax.rsqrt(squares / (HEADS * HEAD_DIM) + 1e-06)
+    write(early, 0)
     a_flow.last()
     add_late(opposite)
     a_flow.near(opposite2)
     add_late(opposite2)
-    for b in range(tiles):
-        rows = slice(b * LANES, (b + 1) * LANES)
-        out_ref[rows, :] = (acc_ref[rows, :] * jnp.tile(column(scale[:, rows]), (1, width // LANES))).astype(BF16)
+    write(late, 1)
 
     for n in waiting:
         loads[n].wait()
     for copy in sent:
         copy.wait_send()
+    out_copy(early, 0).wait()
+    out_copy(late, 1).wait()
 
 
 def per_device(query_rows, key_rows, value_rows, log_decay, norm_gain, out_weight):
@@ -477,14 +494,14 @@
     heads = log_decay.shape[0]
     depth, width = out_weight.shape
     hbm = pl.BlockSpec(memory_space=pltpu.HBM)
-    vmem = pl.BlockSpec(memory_space=pltpu.VMEM)
     dma = pltpu.SemaphoreType.DMA
     return pl.pallas_call(
         kernel,
         out_shape=jax.ShapeDtypeStruct((length, width), BF16),
         in_specs=[hbm] * 6,
-        out_specs=vmem,
+        out_specs=hbm,
         scratch_shapes=[
+            pltpu.VMEM((length, width), BF16),
             pltpu.VMEM((heads, length), F32),
             pltpu.VMEM((1, features), F32),
             pltpu.VMEM((length, features), BF16),
@@ -515,7 +532,7 @@
             pltpu.VMEM((EARLY, features), BF16),
             pltpu.VMEM((length, LANES), F32),
             pltpu.VMEM((8, 1, length), F32),
-            dma((6,)),
+            dma((2,)), dma((6,)),
             dma((NZ,)), dma((NZ,)), dma((NZ,)), dma((NZ,)),
             dma((7,)), dma((7,)), dma((7,)), dma((7,)),
             dma((NY,)), dma((NY,)), dma((NY,)), dma((NY,)),

time: 56 us -> 55.7 us (level)
  no operation moved by 1% of the time
where the time goes in v3:
time: 55.7 us; the launch traced here: 55.5 us
  Pallas kernels  53.7 us (96%)
  local copies, waits for them, and re-layouts  1.78 us (3%)
    pallas_call x1, Pallas kernels, per_device(): pl.pallas_call(kernel, out_shape=jax.ShapeDtypeStruct((length, width), BF...  53.7 us
    unnamed x1, local copies, waits for them, and re-layouts  1.78 us

profile of v3, /device:TPU:1, one launch (start us, length us, event | category | flops | bytes accessed | tf_op | source)
XLA Modules:
  0.0 55.5 jit_solution(10088060220402576553)
XLA Ops:
  0.0 53.7 %attention_layer.1 = bf16[512,384]{1,0:T(8,128)(2,1)} custom-call(bf16[512,512]{1,0:T(8,128)(2,1)} %q_hbm.1, bf16[512,512]{1,0:T(8,128)(2,1)} %k_hbm.1, bf16[512,512]{1,0:T(8,128)(2,1)} %v_hbm.1, f32[4,512]{1,0:T(4,128)} %ld_hbm.1, f32[1,512]{1,0:T(1,128)} %bitcast.1, bf16[4096,384]{1,0:T(8,128)(2,1)} %w_hbm.1), custom_call_target="tpu_custom_call" | custom-call | tf_op jit(solution)/shard_map/attention_layer/pallas_call | solution.py:498
  53.7 1.8 %copy.8 = bf16[512,384]{1,0:T(8,128)(2,1)} copy(bf16[512,384]{1,0:T(8,128)(2,1)} %attention_layer.1) | data formatting | bytes 786432

commit v4 on v3

--- a/solution.py
+++ b/solution.py
@@ -435,9 +435,9 @@
     al_flow.last()
     a_flow.near(partner)
     add_late(partner)
+    a_flow.first()
     add_carried(left)
     add_carried(right)
-    a_flow.first()
     a_flow.second()
     add_late(left)
     add_late(right)

time: 55.7 us -> 55.7 us (level)
  no operation moved by 1% of the time
where the time goes in v4:
time: 55.7 us; the launch traced here: 55.5 us
  Pallas kernels  53.7 us (96%)
  local copies, waits for them, and re-layouts  1.78 us (3%)
    pallas_call x1, Pallas kernels, per_device(): pl.pallas_call(kernel, out_shape=jax.ShapeDtypeStruct((length, width), BF...  53.7 us
    unnamed x1, local copies, waits for them, and re-layouts  1.78 us

profile of v4, /device:TPU:1, one launch (start us, length us, event | category | flops | bytes accessed | tf_op | source)
XLA Modules:
  0.0 55.5 jit_solution(9657157344850910175)
XLA Ops:
  0.0 53.7 %attention_layer.1 = bf16[512,384]{1,0:T(8,128)(2,1)} custom-call(bf16[512,512]{1,0:T(8,128)(2,1)} %q_hbm.1, bf16[512,512]{1,0:T(8,128)(2,1)} %k_hbm.1, bf16[512,512]{1,0:T(8,128)(2,1)} %v_hbm.1, f32[4,512]{1,0:T(4,128)} %ld_hbm.1, f32[1,512]{1,0:T(1,128)} %bitcast.1, bf16[4096,384]{1,0:T(8,128)(2,1)} %w_hbm.1), custom_call_target="tpu_custom_call" | custom-call | tf_op jit(solution)/shard_map/attention_layer/pallas_call | solution.py:498
  53.7 1.8 %copy.8 = bf16[512,384]{1,0:T(8,128)(2,1)} copy(bf16[512,384]{1,0:T(8,128)(2,1)} %attention_layer.1) | data formatting | bytes 786432

commit v5 on v3

--- a/solution.py
+++ b/solution.py
@@ -16,7 +16,7 @@
 NZ = 16
 NY = 4
 NX = 4
-EARLY = 288
+EARLY = 320
 FAR = (8, 7, 9, 6, 10, 5, 11)
 NEAR = (4, 12, 3, 13, 2, 14, 1, 15)
 FAR_FIRST = FAR + NEAR

time: 55.7 us -> 56 us (level)
  no operation moved by 1% of the time
where the time goes in v5:
time: 56 us; the launch traced here: 55.8 us
  Pallas kernels  54 us (96%)
  local copies, waits for them, and re-layouts  1.78 us (3%)
    pallas_call x1, Pallas kernels, per_device(): pl.pallas_call(kernel, out_shape=jax.ShapeDtypeStruct((length, width), BF...  54 us
    unnamed x1, local copies, waits for them, and re-layouts  1.78 us

profile of v5, /device:TPU:1, one launch (start us, length us, event | category | flops | bytes accessed | tf_op | source)
XLA Modules:
  0.0 55.8 jit_solution(12187677329467614515)
XLA Ops:
  0.0 54.0 %attention_layer.1 = bf16[512,384]{1,0:T(8,128)(2,1)} custom-call(bf16[512,512]{1,0:T(8,128)(2,1)} %q_hbm.1, bf16[512,512]{1,0:T(8,128)(2,1)} %k_hbm.1, bf16[512,512]{1,0:T(8,128)(2,1)} %v_hbm.1, f32[4,512]{1,0:T(4,128)} %ld_hbm.1, f32[1,512]{1,0:T(1,128)} %bitcast.1, bf16[4096,384]{1,0:T(8,128)(2,1)} %w_hbm.1), custom_call_target="tpu_custom_call" | custom-call | tf_op jit(solution)/shard_map/attention_layer/pallas_call | solution.py:498
  54.0 1.8 %copy.8 = bf16[512,384]{1,0:T(8,128)(2,1)} copy(bf16[512,384]{1,0:T(8,128)(2,1)} %attention_layer.1) | data formatting | bytes 786432
